TPU v7x, 512 devices: a whole 4x8x8 slice. The times are simulated.
512 devices in a mesh: vocab: 64 (over x, y, core), hid: 8 (over z).
Axes of the slice: x: 4, y: 8, z: 8, core: 2. Of those that a mesh axis runs over, the one named last changes fastest.
Arguments:
- hidden_states: bfloat16 [768, 8192], P('vocab', 'hid'), may hold values from -10 to 10
- head_weight: bfloat16 [8192, 81920], P('hid', 'vocab'), may hold values from -8 to 8
- focus_tiles: int32 [4096, 2], P('vocab'), may hold values from 0 to 767, as said below
- focus_blocks: bfloat16 [4096, 128, 128], P('vocab'), may hold values from -0.5 to 0.5
Outputs:
- student_target: float32 [768, 98304], P('hid', 'vocab')
Inputs may be any that keep to these rules, and one draw needn't show every extreme that they name: `focus_tiles`: rows k * 64 to (k + 1) * 64 - 1 name teacher tiles k * 10 to (k + 1) * 10 - 1 in column 0; column 1 is a student tile, whose owner is the tile divided by 12. Within each such block of rows no owner is named more than 2 times, and one owner, drawn from the seed, is named exactly 2 times in every block; other owners may be named 2 times as well.
All inputs are finite; a program needn't handle non-finite values.
Results may differ from a plain program's by a relative error of at most 0.0035.
Values may be sent and summed in bfloat16 or wider, within the bound.
A program may use at most 64 MiB of HBM per device.

v0:
```python
import jax
import jax.numpy as jnp
from jax import lax
from jax.sharding import PartitionSpec as P

TILE = 128
STILES_DEV = 12
CAP = 2


def sent_to_all(shard, axis):
    size = lax.axis_size(axis)
    return lax.all_to_all(
        jnp.broadcast_to(shard[None], (size, *shard.shape)), axis, 0, 0, tiled=True
    )


def joined_along(tiles, dim):
    lengths = list(tiles.shape[1:])
    lengths[dim] *= tiles.shape[0]
    return jnp.moveaxis(tiles, 0, dim).reshape(lengths)


def gather_directly(shard, axis, dim):
    tiles = sent_to_all(shard, axis)
    return joined_along(tiles, dim)


def all_in_one(shard, axis):
    leaves = jax.tree.leaves(shard)
    turns = sorted(range(len(leaves)), key=lambda k: -leaves[k].size)
    width = (1, *leaves[turns[0]].shape)[-1]
    lines = [
        jnp.pad(leaves[k].reshape(-1), (0, -leaves[k].size % width)).reshape(-1, width)
        for k in turns
    ]
    both, at, found = (sent_to_all(jnp.concatenate(lines), axis), 0, {})
    for k, line in zip(turns, lines):
        piece = both[:, at : at + len(line)].reshape(len(both), -1)
        found[k] = piece[:, : leaves[k].size].reshape(-1, *leaves[k].shape)
        at += len(line)
    numbers = iter(range(len(leaves)))
    return jax.tree.map(lambda _: found[next(numbers)], shard)


def joined_by_halves(pieces, combine):
    while len(jax.tree.leaves(pieces)[0]) > 1:
        pieces = jax.vmap(combine)(
            *(jax.tree.map(lambda part: part[side::2], pieces) for side in (0, 1))
        )
    return jax.tree.map(lambda part: part[0], pieces)


def joined_all(shard, axis, combine):
    pieces = all_in_one(shard, axis)
    return joined_by_halves(pieces, combine)


def side_by_side(arrays, axis, split_dim, concat_dim, along):
    columns = [a.reshape(*a.shape[:along], -1) for a in arrays]
    both = jnp.concatenate(columns, axis=along)
    whole, at, gathered = (
        lax.all_to_all(both, axis, split_axis=split_dim, concat_axis=concat_dim, tiled=True),
        0,
        [],
    )
    for a, column in zip(arrays, columns):
        piece = whole[..., at : at + column.shape[along]]
        gathered.append(piece.reshape(*piece.shape[:along], *a.shape[along:]))
        at += column.shape[along]
    return tuple(gathered)


def combine_parts(earlier, later):
    first_top, first_sum = earlier
    second_top, second_sum = later
    joined = jnp.maximum(first_top, second_top)
    return (
        joined,
        first_sum * jnp.exp(first_top - joined) + second_sum * jnp.exp(second_top - joined),
    )


def per_device(hidden_states, head_weight, focus_tiles, focus_blocks):
    hid_count = lax.axis_size("hid")
    vocab_count = lax.axis_size("vocab")
    gathered = gather_directly(hidden_states, "vocab", 0)
    row_count = gathered.shape[0] // hid_count
    logits = lax.psum_scatter(
        jnp.dot(gathered, head_weight, preferred_element_type=jnp.float32),
        "hid",
        scatter_dimension=0,
        tiled=True,
    )
    local_top = jnp.max(logits, axis=1)
    local_values = jnp.exp(logits - local_top[:, None])
    local_sum = jnp.sum(local_values, axis=1)
    row_top, denominator = joined_all((local_top, local_sum), "vocab", combine_parts)
    exp_values = local_values * jnp.exp(local_top - row_top)[:, None]
    weights = exp_values.astype(jnp.bfloat16)
    tiles_here = weights.shape[1] // TILE
    prob_tiles = weights.reshape(row_count, tiles_here, TILE)
    entry_count = focus_tiles.shape[0]
    local_teacher = focus_tiles[:, 0] - lax.axis_index("vocab") * tiles_here
    selector = (local_teacher[:, None] == jnp.arange(tiles_here, dtype=jnp.int32)[None, :]).astype(
        jnp.bfloat16
    )
    chosen = jnp.einsum(
        "et,rtk->erk", selector, prob_tiles, preferred_element_type=jnp.float32
    ).astype(jnp.bfloat16)
    partials = jnp.einsum("erk,ekc->erc", chosen, focus_blocks, preferred_element_type=jnp.float32)
    owner_index = focus_tiles[:, 1] // STILES_DEV
    target_tile = focus_tiles[:, 1] % STILES_DEV
    positions_idx = jnp.arange(entry_count, dtype=jnp.int32)
    same_owner = (owner_index[:, None] == owner_index[None, :]) & (
        positions_idx[None, :] < positions_idx[:, None]
    )
    slot_rank = jnp.sum(same_owner.astype(jnp.int32), axis=1)
    destination = owner_index * CAP + slot_rank
    placement_map = (
        destination[:, None] == jnp.arange(vocab_count * CAP, dtype=jnp.int32)[None, :]
    ).astype(jnp.float32)
    outgoing = jnp.einsum("ed,erc->drc", placement_map, partials, precision=lax.Precision.HIGHEST)
    outgoing = outgoing.reshape(vocab_count, CAP, row_count, TILE)
    tile_labels = jnp.einsum(
        "ed,e->d",
        placement_map,
        target_tile.astype(jnp.float32) + 1.0,
        precision=lax.Precision.HIGHEST,
    )
    tile_labels = tile_labels.reshape(vocab_count, CAP)
    arrived, arrived_labels = side_by_side((outgoing, tile_labels), "vocab", 0, 0, 2)
    received = arrived.reshape(vocab_count * CAP, row_count, TILE)
    tile_match = (
        arrived_labels.reshape(-1)[:, None]
        == (jnp.arange(STILES_DEV, dtype=jnp.float32) + 1.0)[None, :]
    ).astype(jnp.float32)
    mapped = jnp.einsum("sj,src->rjc", tile_match, received, precision=lax.Precision.HIGHEST)
    mapped = mapped.reshape(row_count, STILES_DEV * TILE)
    student_size = STILES_DEV * TILE * vocab_count
    return student_size * mapped / denominator[:, None]


def solution(mesh):
    return jax.shard_map(
        per_device,
        mesh=mesh,
        in_specs=(P("vocab", "hid"), P("hid", "vocab"), P("vocab", None), P("vocab", None, None)),
        out_specs=P("hid", "vocab"),
        check_vma=False,
    )
```

profile of v0, /device:TPU:1, one launch (start us, length us, event | category | flops | bytes accessed | tf_op | source)
XLA Modules:
  0.0 372.4 jit_solution(1069940598575100857)
XLA Ops:
  6.5 0.0 copy-start
  6.5 0.0 reduce-scatter.2.cloned.1.call-start
  6.5 1.2 broadcast_in_dim.4
  7.7 62.7 %all_to_all.15 = bf16[64,12,1024]{2,1,0:T(8,128)(2,1)} all-to-all(bf16[64,12,1024]{2,1,0:T(8,128)(2,1)S(1)} %broadcast_in_dim.4), channel_id=1, replica_groups=mesh['vocab'=64,'hid'=8] {'vocab'}, dimensions={0} | all-to-all | bytes 3145728 | tf_op jit(solution)/shard_map/all_to_all | solution.py:13
  70.4 3.6 reshape.93
  74.0 0.0 copy-done
  74.0 5.5 %fusion.39 = f32[768,1280]{1,0:T(8,128)} fusion(bf16[768,1024]{1,0:T(8,128)(2,1)} %reshape.93, bf16[1024,1280]{1,0:T(8,128)(2,1)S(1)} %copy-done), kind=kOutput, calls=%fused_computation.62 | convolution fusion | flops 2013265920 | bytes 8126464 | tf_op jit(solution)/shard_map/dot_general | solution.py:90
  79.5 0.0 copy-start.1
  79.5 0.0 reduce-scatter.2.cloned.1.call-update
  79.6 0.6 copy-done.1
  80.2 0.2 convert_reduce_fusion
  80.4 0.1 broadcast_compare_fusion
  80.6 55.1 %reduce-scatter.2.cloned.1.call-done = f32[96,1280]{1,0:T(8,128)} async-done(((f32[768,1280]{1,0:T(8,128)}), f32[96,1280]{1,0:T(8,128)}) %reduce-scatter.2.cloned.1.call-update) | async-done | bytes 491536 | tf_op jit(solution)/shard_map/reduce_scatter | solution.py:89
  135.6 1.2 reduce_max.9
  136.8 1.3 fusion.9
  138.1 0.7 broadcast_in_dim.5
  138.7 10.5 %all-to-all-start.1 = ((f32[64,2,96]{2,1,0:T(2,128)}), f32[64,2,96]{2,1,0:T(2,128)S(1)}, u32[]{:S(2)}, u32[]{:S(2)}) async-start(f32[64,2,96]{2,1,0:T(2,128)} %broadcast_in_dim.5), calls=%async_computation.2 | async-start | bytes 131072 | tf_op jit(solution)/shard_map/all_to_all | solution.py:13
  149.2 0.1 fusion.10
  149.3 0.2 copy.24
  149.5 9.4 %all-to-all-done.1 = f32[64,2,96]{2,1,0:T(2,128)S(1)} async-done(((f32[64,2,96]{2,1,0:T(2,128)}), f32[64,2,96]{2,1,0:T(2,128)S(1)}, u32[]{:S(2)}, u32[]{:S(2)}) %all-to-all-start.1) | async-done | bytes 49184 | tf_op jit(solution)/shard_map/all_to_all | solution.py:13
  159.0 0.1 fusion.38
  159.5 1.2 multiply_convert_fusion
  160.7 0.2 copy.19
  160.9 0.4 copy.20
  161.3 0.6 convolution_convert_fusion
  161.9 3.1 fusion.4
  165.0 4.8 %fusion.2 = f32[128,96,128]{2,0,1:T(8,128)S(1)} fusion(f32[64,96,128]{2,1,0:T(8,128)S(1)} %fusion.4, s32[64]{0:T(128)S(1)} %fusion.28), kind=kOutput, calls=%fused_computation.3 | convolution fusion | flops 1207967744 | bytes 9437440 | tf_op jit(solution)/shard_map/ed,erc->drc/dot_general | solution.py:123
  169.8 6.3 %copy.23 = f32[128,96,128]{2,1,0:T(8,128)} copy(f32[128,96,128]{2,0,1:T(8,128)S(1)} %fusion.2) | data formatting | bytes 12582912 | tf_op jit(solution)/shard_map/ed,erc->drc/dot_general | solution.py:123
  176.1 8.6 %reshape_reshape.7 = f32[64,2,12288]{2,1,0:T(2,128)} reshape(f32[128,96,128]{2,1,0:T(8,128)} %copy.23) | data formatting | bytes 12582912 | tf_op jit(solution)/shard_map/reshape;reshape | solution.py:60
  184.7 8.7 %pad_maximum_fusion = f32[64,2,12289]{2,1,0:T(2,128)} fusion(f32[64,2,1]{2,1,0:T(2,128)S(1)} %copy.24, f32[64,2,12288]{2,1,0:T(2,128)} %reshape_reshape.7), kind=kLoop, calls=%fused_computation | loop fusion | flops 1572992 | bytes 12583936 | tf_op jit(solution)/shard_map/concatenate | solution.py:61
  193.4 5.5 %all-to-all-start.2 = ((f32[64,2,12289]{2,1,0:T(2,128)}), f32[64,2,12289]{2,1,0:T(2,128)}, u32[]{:S(2)}, u32[]{:S(2)}) async-start(f32[64,2,12289]{2,1,0:T(2,128)} %pad_maximum_fusion), calls=%async_computation.3 | async-start | bytes 12713984 | tf_op jit(solution)/shard_map/all_to_all | solution.py:63
  198.9 142.2 %all-to-all-done.2 = f32[64,2,12289]{2,1,0:T(2,128)} async-done(((f32[64,2,12289]{2,1,0:T(2,128)}), f32[64,2,12289]{2,1,0:T(2,128)}, u32[]{:S(2)}, u32[]{:S(2)}) %all-to-all-start.2) | async-done | bytes 6292000 | tf_op jit(solution)/shard_map/all_to_all | solution.py:63
  341.1 1.0 slice_reduce_fusion
  342.1 0.1 eq.104
  342.2 6.2 %slice.126 = f32[64,2,12288]{2,1,0:T(2,128)} slice(f32[64,2,12289]{2,1,0:T(2,128)} %all-to-all-done.2), slice={[0:64], [0:2], [0:12288]} | slice | bytes 12582912 | tf_op jit(solution)/shard_map/slice | solution.py:68
  348.4 9.4 %reshape_reshape.8 = f32[128,96,128]{2,1,0:T(8,128)} reshape(f32[64,2,12288]{2,1,0:T(2,128)} %slice.126) | data formatting | bytes 12582912 | tf_op jit(solution)/shard_map/reshape;reshape | solution.py:133
  357.8 6.7 %fusion.6 = f32[96,128,12]{1,2,0:T(8,128)S(1)} fusion(f32[128,96,128]{2,1,0:T(8,128)} %reshape_reshape.8, f32[128]{0:T(128)S(1)} %eq.104, f32[12]{0:T(128)S(1)} %iota_add_fusion), kind=kOutput, calls=%fused_computation.8 | convolution fusion | flops 226641408 | bytes 6881840 | tf_op jit(solution)/shard_map/sj,src->rjc/dot_general | solution.py:138
  364.5 1.0 bitcast_divide_fusion
  (33 shorter events, 0.5 us)
Async XLA Ops:
  6.5 67.5 %copy-start = (bf16[1024,1280]{1,0:T(8,128)(2,1)S(1)}, bf16[1024,1280]{1,0:T(8,128)(2,1)}, u32[]{:S(2)}) copy-start(bf16[1024,1280]{1,0:T(8,128)(2,1)} %param.5) | copy-start | bytes 7864324
  6.5 129.1 %reduce-scatter.2.cloned.1.call-start = ((), (), s32[]{:S(2)}) async-start(), calls=%async_computation.4 | async-start | bytes 4423680 | tf_op jit(solution)/shard_map/reduce_scatter | solution.py:89
  79.5 0.7 copy-start.1
  138.7 20.2 %all-to-all-start.1 = ((f32[64,2,96]{2,1,0:T(2,128)}), f32[64,2,96]{2,1,0:T(2,128)S(1)}, u32[]{:S(2)}, u32[]{:S(2)}) async-start(f32[64,2,96]{2,1,0:T(2,128)} %broadcast_in_dim.5), calls=%async_computation.2 | async-start | bytes 131072 | tf_op jit(solution)/shard_map/all_to_all | solution.py:13
  193.4 147.7 %all-to-all-start.2 = ((f32[64,2,12289]{2,1,0:T(2,128)}), f32[64,2,12289]{2,1,0:T(2,128)}, u32[]{:S(2)}, u32[]{:S(2)}) async-start(f32[64,2,12289]{2,1,0:T(2,128)} %pad_maximum_fusion), calls=%async_computation.3 | async-start | bytes 12713984 | tf_op jit(solution)/shard_map/all_to_all | solution.py:63
Sparse Core Ops, SparseCore 0:
  79.7 55.9 reduce-scatter.1
where the time goes:
time: 373 us; the launch traced here: 372 us
  waiting for transfers between devices  207 us (55%)
  blocking collectives  62.7 us (17%)
  local copies, waits for them, and re-layouts  38.8 us (10%)
  matrix products  20.8 us (6%)
  starting transfers between devices  15.9 us (4%)
  other arithmetic  13.8 us (4%)
  between operations  13.6 us (4%)
    all_to_all x1, waiting for transfers between devices, side_by_side(): lax.all_to_all(both, axis, split_axis=split_dim, concat_axis=concat_dim,...  142 us
    all_to_all x1, blocking collectives, sent_to_all(): lax.all_to_all(jnp.broadcast_to(shard[None], (size, *shard.shape)), axis,...  62.7 us
    reduce_scatter x1, waiting for transfers between devices, per_device(): lax.psum_scatter(jnp.dot(gathered, head_weight, preferred_element_type=jn...  55.1 us
    all_to_all x1, starting transfers between devices, sent_to_all(): lax.all_to_all(jnp.broadcast_to(shard[None], (size, *shard.shape)), axis,...  10.5 us
    all_to_all x1, waiting for transfers between devices, sent_to_all(): lax.all_to_all(jnp.broadcast_to(shard[None], (size, *shard.shape)), axis,...  9.42 us
    another operation x1, local copies, waits for them, and re-layouts, per_device(): received = arrived.reshape(vocab_count * CAP, row_count, TILE)  9.36 us
    concatenate x1, other arithmetic, side_by_side(): both = jnp.concatenate(columns, axis=along)  8.71 us
    another operation x1, local copies, waits for them, and re-layouts, side_by_side(): columns = [a.reshape(*a.shape[:along], -1) for a in arrays]  8.58 us
  transfers between devices with their start and end apart: 3, of which 3 were waited for; matrix products, arithmetic and copies ran while one was open for 0% of the time, Pallas kernels for 0%

commit v1 on v0

v1 whole, which is shorter than its diff:
```python
import functools

import jax
import jax.numpy as jnp
from jax import lax
from jax.experimental import pallas as pl
from jax.experimental.pallas import tpu as pltpu
from jax.sharding import PartitionSpec as P

TILE = 128
STILES = 12
CAP = 2
NX, NY, NC, NZ = 4, 8, 2, 8
MESH = pl.DeviceIdType.MESH
VMEM_LIMIT = 60 * 1024 * 1024
ORDER = (4, 3, -3, 2, -2, 1, -1, 0)
F32, BF16, I16, I32 = jnp.float32, jnp.bfloat16, jnp.int16, jnp.int32
TINY = 1e-30
FULL = 32767.0


def index_of(x, y, c):
    return (x * NY + y) * NC + c


def my_place():
    v = lax.axis_index("vocab")
    return v // (NY * NC), (v // NC) % NY, v % NC


def to_vocab(x, y, c):
    return {"vocab": index_of(x, y, c)}


def signal_all(peers):
    barrier = pltpu.get_barrier_semaphore()
    for peer in peers:
        pl.semaphore_signal(barrier, inc=1, device_id=peer, device_id_type=MESH)
    pl.semaphore_wait(barrier, len(peers))


def remote(src, dst, send_sem, recv_sem, peer):
    return pltpu.make_async_remote_copy(
        src_ref=src, dst_ref=dst, send_sem=send_sem, recv_sem=recv_sem,
        device_id=peer, device_id_type=MESH,
    )


def coded(value):
    top = jnp.maximum(jnp.max(jnp.abs(value), axis=1, keepdims=True), TINY)
    codes = jnp.round(value * (FULL / top)).astype(I32).astype(I16)
    return codes, top * (1.0 / FULL)


def lane_is(shape, lane):
    return lax.broadcasted_iota(I32, shape, 1) == lane


def ring_halves(step, side):
    if step == 0:
        return (0,) if side == 0 else (1,)
    return (0, 1)


def gather_logits_kernel(
    hid_ref, w_hbm, out_ref, w_ref, all_ref, part_ref,
    out_code, in_code, out_scale, in_scale,
    w_sem, own_sem, ysend, yrecv, xsend, xrecv, rsend, rrecv, csend, crecv,
    zsend, zrecv, zssend, zsrecv,
):
    x, y, c = my_place()
    z = lax.axis_index("hid")
    load_w = pltpu.make_async_copy(w_hbm, w_ref, w_sem)
    load_w.start()
    xs = ((x + 1) % NX, (x + NX - 1) % NX)
    zs = ((z + 1) % NZ, (z + NZ - 1) % NZ)
    peers = [to_vocab(x, (y + d) % NY, c) for d in range(1, NY)]
    peers += [to_vocab(n, y, c) for n in xs] + [to_vocab(x, y, 1 - c)]
    peers += [{"hid": n} for n in zs]
    signal_all(peers)

    me = index_of(x, y, c)
    sent = []
    arrived = {}

    def send(src, block, send_sem, recv_sem, peer):
        copy = remote(src, all_ref.at[block], send_sem, recv_sem, peer)
        copy.start()
        sent.append(copy)
        return copy

    for d in (4, 3, 5, 2, 6, 1, 7):
        arrived["y", d] = send(
            hid_ref, me, ysend.at[d], yrecv.at[d], to_vocab(x, (y + d) % NY, c)
        )
    own = pltpu.make_async_copy(hid_ref, all_ref.at[me], own_sem)
    own.start()
    for d in (0, 1, 7, 2, 6, 3, 5, 4):
        block = index_of(x, (y + NY - d) % NY, c)
        src = all_ref.at[block]
        if d == 0:
            src = hid_ref
        else:
            arrived["y", d].wait_recv()
        for side in (0, 1):
            arrived["x", side, d] = send(
                src, block, xsend.at[side, d], xrecv.at[side, d], to_vocab(xs[side], y, c)
            )
        arrived["c", 0, d] = send(
            src, block, csend.at[0, d], crecv.at[0, d], to_vocab(x, y, 1 - c)
        )
    for d in (0, 1, 7, 2, 6, 3, 5, 4):
        for side in (0, 1):
            arrived["x", side, d].wait_recv()
            block = index_of(xs[1 - side], (y + NY - d) % NY, c)
            src = all_ref.at[block]
            if d % 2 == side:
                arrived["r", d] = send(
                    src, block, rsend.at[d], rrecv.at[d], to_vocab(xs[side], y, c)
                )
            arrived["c", 1 + side, d] = send(
                src, block, csend.at[1 + side, d], crecv.at[1 + side, d],
                to_vocab(x, y, 1 - c),
            )
    for d in (0, 1, 7, 2, 6, 3, 5, 4):
        arrived["r", d].wait_recv()
        block = index_of((x + 2) % NX, (y + NY - d) % NY, c)
        arrived["c", 3, d] = send(
            all_ref.at[block], block, csend.at[3, d], crecv.at[3, d],
            to_vocab(x, y, 1 - c),
        )
    own.wait()
    load_w.wait()
    for kind in range(4):
        for d in range(NY):
            arrived["c", kind, d].wait_recv()

    columns = 256

    def partial(k):
        target = (z + ORDER[k] + NZ) % NZ
        rows = all_ref[pl.ds(target * 8, 8)].reshape(128, all_ref.shape[2])

        def body(n, carry):
            at = pl.ds(pl.multiple_of(n * columns, columns), columns)
            p = jnp.dot(rows, w_ref[:, at], preferred_element_type=F32)
            for i in range(4):
                q = p[32 * i : 32 * i + 32]
                part_ref[k, pl.ds(24 * i, 8), at] = q[0:8]
                part_ref[k, pl.ds(24 * i + 8, 8), at] = q[16:24]
                part_ref[k, pl.ds(24 * i + 16, 8), at] = q[8:16] + pltpu.roll(q[24:32], 4, 0)
            return carry

        lax.fori_loop(0, w_ref.shape[1] // columns, body, 0)

    def decoded(side, step, half, g):
        scale = in_scale[side, step, half][:, g : g + 1]
        return in_code[side, step, half, pl.ds(16 * g, 16), :].astype(F32) * scale

    hops = {}

    def wait_hop(side, step, half):
        for copy in hops[side, step, half]:
            copy.wait_recv()

    def hop(side, step, half, k):
        has_input = step >= 1 and half in ring_halves(step - 1, side)
        if has_input:
            wait_hop(side, step - 1, half)
        scales = jnp.zeros((16, 128), F32)
        for g in range(3):
            value = part_ref[k, pl.ds(48 * half + 16 * g, 16), :]
            if has_input:
                value = value + decoded(side, step - 1, half, g)
            codes, scale = coded(value)
            out_code[side, step, half, pl.ds(16 * g, 16), :] = codes
            scales = jnp.where(lane_is((16, 128), g), scale, scales)
        out_scale[side, step, half] = scales
        peer = {"hid": zs[side]}
        copies = (
            remote(out_scale.at[side, step, half], in_scale.at[side, step, half],
                   zssend.at[side, step, half], zsrecv.at[side, step, half], peer),
            remote(out_code.at[side, step, half], in_code.at[side, step, half],
                   zsend.at[side, step, half], zrecv.at[side, step, half], peer),
        )
        for copy in copies:
            copy.start()
            sent.append(copy)
        hops[side, step, half] = copies

    partial(0)
    for step in range(4):
        for half in (0, 1):
            for side in (0, 1):
                if half in ring_halves(step, side):
                    hop(side, step, half, 0 if step == 0 else 2 * step - 1 + side)
        if step < 3:
            partial(2 * step + 1)
            partial(2 * step + 2)
    partial(7)
    for half in (0, 1):
        for side in (0, 1):
            wait_hop(side, 3, half)
        for g in range(3):
            at = pl.ds(48 * half + 16 * g, 16)
            out_ref[at, :] = (
                part_ref[7, at, :] + decoded(0, 3, half, g) + decoded(1, 3, half, g)
            )
    for copy in sent:
        copy.wait_send()


def gather_logits(hidden, head_weight):
    depth, width = head_weight.shape
    dma = pltpu.SemaphoreType.DMA
    return pl.pallas_call(
        gather_logits_kernel,
        out_shape=jax.ShapeDtypeStruct((96, width), F32),
        in_specs=[
            pl.BlockSpec(memory_space=pltpu.VMEM),
            pl.BlockSpec(memory_space=pl.ANY),
        ],
        out_specs=pl.BlockSpec(memory_space=pltpu.VMEM),
        scratch_shapes=[
            pltpu.VMEM((depth, width), BF16),
            pltpu.VMEM((NX * NY * NC, 16, depth), BF16),
            pltpu.VMEM((8, 96, width), F32),
            pltpu.VMEM((2, 4, 2, 48, width), I16),
            pltpu.VMEM((2, 4, 2, 48, width), I16),
            pltpu.VMEM((2, 4, 2, 16, 128), F32),
            pltpu.VMEM((2, 4, 2, 16, 128), F32),
            dma, dma, dma((NY,)), dma((NY,)), dma((2, NY)), dma((2, NY)),
            dma((NY,)), dma((NY,)), dma((4, NY)), dma((4, NY)),
            dma((2, 4, 2)), dma((2, 4, 2)), dma((2, 4, 2)), dma((2, 4, 2)),
        ],
        compiler_params=pltpu.CompilerParams(
            collective_id=0, has_side_effects=True, vmem_limit_bytes=VMEM_LIMIT
        ),
        name="gather_logits",
    )(hidden, head_weight)


def map_tiles_kernel(tiles_ref, logits_ref, blocks_ref, slots_ref, meta_ref, weights_ref, count_ref):
    teacher_tiles = logits_ref.shape[1] // TILE
    first = lax.axis_index("vocab") * teacher_tiles
    stats = jnp.zeros((6, 16, 128), F32)
    pieces = []
    for g in range(6):
        rows = pl.ds(16 * g, 16)
        logits = logits_ref[rows, :]
        top = jnp.max(logits, axis=1, keepdims=True)
        values = jnp.exp(logits - top)
        total = jnp.sum(values, axis=1, keepdims=True)
        for t in range(teacher_tiles):
            weights_ref[t, rows, :] = values[:, t * TILE : (t + 1) * TILE].astype(BF16)
        pieces.append((top, total))
    stats = jnp.zeros((16, 128), F32)
    for g, (top, total) in enumerate(pieces):
        stats = jnp.where(lane_is((16, 128), g), top, stats)
        stats = jnp.where(lane_is((16, 128), 8 + g), total, stats)
    for d in range(8):
        meta_ref[d, 0:16, :] = jnp.full((16, 128), -1.0, F32)
        meta_ref[d, 16:32, :] = stats

    def clear(i, carry):
        slots_ref[i] = jnp.zeros((96, TILE), BF16)
        return carry

    lax.fori_loop(0, slots_ref.shape[0], clear, 0)

    def clear_count(i, carry):
        count_ref[i] = 0
        return carry

    lax.fori_loop(0, count_ref.shape[0], clear_count, 0)

    def entry(e, carry):
        student = tiles_ref[e, 1]
        owner = student // STILES
        label = student - owner * STILES
        rank = count_ref[owner]
        count_ref[owner] = rank + 1
        group = (owner // (NY * NC)) * NC + owner % NC
        line = ((owner // NC) % NY) * CAP + rank
        product = jnp.dot(
            weights_ref[tiles_ref[e, 0] - first], blocks_ref[e], preferred_element_type=F32
        )
        slots_ref[group * (NY * CAP) + line] = product.astype(BF16)
        meta_ref[group, pl.ds(line, 1), :] = jnp.full((1, 128), label.astype(F32))
        return carry

    lax.fori_loop(0, tiles_ref.shape[0], entry, 0, unroll=4)


def map_tiles(focus_tiles, logits, focus_blocks):
    groups = NX * NC
    return pl.pallas_call(
        map_tiles_kernel,
        out_shape=(
            jax.ShapeDtypeStruct((groups * NY * CAP, 96, TILE), BF16),
            jax.ShapeDtypeStruct((groups, 32, 128), F32),
        ),
        in_specs=[
            pl.BlockSpec(memory_space=pltpu.SMEM),
            pl.BlockSpec(memory_space=pltpu.VMEM),
            pl.BlockSpec(memory_space=pltpu.VMEM),
        ],
        out_specs=(
            pl.BlockSpec(memory_space=pltpu.VMEM),
            pl.BlockSpec(memory_space=pltpu.VMEM),
        ),
        scratch_shapes=[
            pltpu.VMEM((logits.shape[1] // TILE, 96, TILE), BF16),
            pltpu.SMEM((NX * NY * NC,), I32),
        ],
        compiler_params=pltpu.CompilerParams(vmem_limit_bytes=VMEM_LIMIT),
        name="map_tiles",
    )(focus_tiles, logits, focus_blocks)


def exchange_kernel(
    slots_hbm, meta_hbm, out_ref, slots_in, meta_in, factor_ref, group_ref, done_ref,
    out_code, in_code, out_stat, in_stat,
    ssend, srecv, msend, mrecv, ysend, yrecv, tsend, trecv,
):
    x, y, c = my_place()
    width = STILES * TILE
    ys = ((y + 1) % NY, (y + NY - 1) % NY)

    def place(o):
        return (x + o // 2) % NX, (c + o % 2) % NC

    peers = []
    for o in range(1, 8):
        px, pc = place(o)
        peers.append(to_vocab(px, y, pc))
    peers += [to_vocab(x, n, c) for n in ys]
    signal_all(peers)

    sent = []
    came = {}
    for o in range(8):
        px, pc = place(o)
        src = meta_hbm.at[px * NC + pc]
        if o == 0:
            copy = pltpu.make_async_copy(src, meta_in.at[0], mrecv.at[0])
        else:
            copy = remote(src, meta_in.at[o], msend.at[o], mrecv.at[o], to_vocab(px, y, pc))
            sent.append(copy)
        copy.start()
        came["m", o] = copy
    for k in range(8):
        row = (y + ORDER[k] + NY) % NY
        for o in (4, 5, 2, 6, 3, 7, 1, 0):
            px, pc = place(o)
            src = slots_hbm.at[pl.ds(((px * NC + pc) * NY + row) * CAP, CAP)]
            if o == 0:
                copy = pltpu.make_async_copy(src, slots_in.at[k, 0], srecv.at[k, 0])
            else:
                copy = remote(
                    src, slots_in.at[k, o], ssend.at[k, o], srecv.at[k, o],
                    to_vocab(px, y, pc),
                )
                sent.append(copy)
            copy.start()
            came[k, o] = copy

    def wait_came(key):
        if key[1] == 0:
            came[key].wait()
        else:
            came[key].wait_recv()

    for o in range(8):
        wait_came(("m", o))
    groups = jnp.zeros((16, 128), F32)
    for g in range(6):
        tops = [meta_in[o, 16:32, g : g + 1] for o in range(8)]
        top = functools.reduce(jnp.maximum, tops)
        total = jnp.zeros((16, 1), F32)
        for o in range(8):
            factor = jnp.exp(tops[o] - top)
            total = total + factor * meta_in[o, 16:32, 8 + g : 9 + g]
            factor_ref[o, pl.ds(16 * g, 16), :] = jnp.broadcast_to(factor, (16, 128))
        groups = jnp.where(lane_is((16, 128), g), top, groups)
        groups = jnp.where(lane_is((16, 128), 8 + g), total, groups)
    group_ref[...] = groups

    def merged(k, at):
        row = (y + ORDER[k] + NY) % NY
        tiles = [jnp.zeros((16, TILE), F32)] * STILES
        for o in range(8):
            factor = factor_ref[o, at, :]
            for i in range(CAP):
                tile = slots_in[k, o, i, at, :].astype(F32) * factor
                label = meta_in[o, pl.ds(row * CAP + i, 1), :]
                for j in range(STILES):
                    tiles[j] = tiles[j] + jnp.where(label == float(j), tile, 0.0)
        return tiles

    hops = {}

    def wait_hop(side, step, half):
        for copy in hops[side, step, half]:
            copy.wait_recv()

    def incoming(side, step, half, g):
        stat = in_stat[side, step, half]
        return stat[:, g : g + 1], stat[:, 8 + g : 9 + g], stat[:, 16 + g : 17 + g]

    def hop(side, step, half, k):
        has_input = step >= 1 and half in ring_halves(step - 1, side)
        if has_input:
            wait_hop(side, step - 1, half)
        stats = jnp.zeros((16, 128), F32)
        for g in range(3):
            row_at = pl.ds(48 * half + 16 * g, 16)
            code_at = pl.ds(16 * g, 16)
            tiles = merged(k, row_at)
            lane = 3 * half + g
            top = group_ref[:, lane : lane + 1]
            total = group_ref[:, 8 + lane : 9 + lane]
            if has_input:
                scale, in_top, in_total = incoming(side, step - 1, half, g)
                new_top = jnp.maximum(top, in_top)
                mine = jnp.exp(top - new_top)
                theirs = jnp.exp(in_top - new_top)
                total = total * mine + in_total * theirs
                scale = scale * theirs
                top = new_top
                for j in range(STILES):
                    code = in_code[side, step - 1, half, code_at, j * TILE : (j + 1) * TILE]
                    tiles[j] = tiles[j] * mine + code.astype(F32) * scale
            codes, scale = coded(jnp.concatenate(tiles, axis=1))
            out_code[side, step, half, code_at, :] = codes
            stats = jnp.where(lane_is((16, 128), g), scale, stats)
            stats = jnp.where(lane_is((16, 128), 8 + g), top, stats)
            stats = jnp.where(lane_is((16, 128), 16 + g), total, stats)
        out_stat[side, step, half] = stats
        peer = to_vocab(x, ys[side], c)
        copies = (
            remote(out_stat.at[side, step, half], in_stat.at[side, step, half],
                   tsend.at[side, step, half], trecv.at[side, step, half], peer),
            remote(out_code.at[side, step, half], in_code.at[side, step, half],
                   ysend.at[side, step, half], yrecv.at[side, step, half], peer),
        )
        for copy in copies:
            copy.start()
            sent.append(copy)
        hops[side, step, half] = copies

    def wait_stage(k):
        for o in range(8):
            wait_came((k, o))

    for step in range(4):
        if step == 0:
            wait_stage(0)
            hop(0, 0, 0, 0)
            hop(1, 0, 1, 0)
        else:
            for side in (0, 1):
                k = 2 * step - 1 + side
                wait_stage(k)
                fresh = 1 if side == 0 else 0
                order = (fresh, 1 - fresh) if step == 1 else (0, 1)
                for half in order:
                    hop(side, step, half, k)
    wait_stage(7)
    for half in (0, 1):
        for side in (0, 1):
            wait_hop(side, 3, half)
        for g in range(3):
            row_at = pl.ds(48 * half + 16 * g, 16)
            code_at = pl.ds(16 * g, 16)
            tiles = merged(7, row_at)
            lane = 3 * half + g
            top = group_ref[:, lane : lane + 1]
            total = group_ref[:, 8 + lane : 9 + lane]
            parts = [incoming(side, 3, half, g) for side in (0, 1)]
            new_top = jnp.maximum(top, jnp.maximum(parts[0][1], parts[1][1]))
            mine = jnp.exp(top - new_top)
            theirs = [jnp.exp(part[1] - new_top) for part in parts]
            total = total * mine + parts[0][2] * theirs[0] + parts[1][2] * theirs[1]
            share = float(width * NX * NY * NC) / total
            for j in range(STILES):
                cols = slice(j * TILE, (j + 1) * TILE)
                value = tiles[j] * mine
                for side in (0, 1):
                    code = in_code[side, 3, half, code_at, cols]
                    value = value + code.astype(F32) * (parts[side][0] * theirs[side])
                done_ref[row_at, cols] = value * share
    early = lax.broadcasted_iota(I32, (8, width), 0) < 4
    for p in range(4):
        second = pltpu.roll(done_ref[24 * p + 8 : 24 * p + 16, :], 4, 0)
        mixed = done_ref[24 * p + 16 : 24 * p + 24, :]
        out_ref[24 * p : 24 * p + 8, :] = done_ref[24 * p : 24 * p + 8, :]
        out_ref[24 * p + 8 : 24 * p + 16, :] = jnp.where(early, mixed, second)
        out_ref[24 * p + 16 : 24 * p + 24, :] = jnp.where(early, second, mixed)
    for copy in sent:
        copy.wait_send()


def exchange(slots, meta):
    width = STILES * TILE
    dma = pltpu.SemaphoreType.DMA
    return pl.pallas_call(
        exchange_kernel,
        out_shape=jax.ShapeDtypeStruct((96, width), F32),
        in_specs=[pl.BlockSpec(memory_space=pl.ANY)] * 2,
        out_specs=pl.BlockSpec(memory_space=pltpu.VMEM),
        scratch_shapes=[
            pltpu.VMEM((8, 8, CAP, 96, TILE), BF16),
            pltpu.VMEM((8, 32, 128), F32),
            pltpu.VMEM((8, 96, TILE), F32),
            pltpu.VMEM((16, 128), F32),
            pltpu.VMEM((96, width), F32),
            pltpu.VMEM((2, 4, 2, 48, width), I16),
            pltpu.VMEM((2, 4, 2, 48, width), I16),
            pltpu.VMEM((2, 4, 2, 16, 128), F32),
            pltpu.VMEM((2, 4, 2, 16, 128), F32),
            dma((8, 8)), dma((8, 8)), dma((8,)), dma((8,)),
            dma((2, 4, 2)), dma((2, 4, 2)), dma((2, 4, 2)), dma((2, 4, 2)),
        ],
        compiler_params=pltpu.CompilerParams(
            collective_id=1, has_side_effects=True, vmem_limit_bytes=VMEM_LIMIT
        ),
        name="exchange",
    )(slots, meta)


def per_device(hidden_states, head_weight, focus_tiles, focus_blocks):
    hidden = jnp.pad(hidden_states, ((0, 16 - hidden_states.shape[0]), (0, 0)))
    logits = gather_logits(hidden, head_weight)
    slots, meta = map_tiles(focus_tiles, logits, focus_blocks)
    return exchange(slots, meta)


def solution(mesh):
    return jax.shard_map(
        per_device,
        mesh=mesh,
        in_specs=(P("vocab", "hid"), P("hid", "vocab"), P("vocab", None), P("vocab", None, None)),
        out_specs=P("hid", "vocab"),
        check_vma=False,
    )
```

time: 373 us -> 128 us (0.34)
  waiting for transfers between devices: 207 us -> 0 us
  Pallas kernels: 0 us -> 123 us
  blocking collectives: 62.7 us -> 0 us
  local copies, waits for them, and re-layouts: 38.8 us -> 4.67 us
  matrix products: 20.8 us -> 0 us
  starting transfers between devices: 15.9 us -> 0 us
  other arithmetic: 13.8 us -> 0 us
  between operations: 13.6 us -> 0.02 us
    all_to_all x2 -> x0, waiting for transfers between devices: 152 us -> none  [the longest x1 142 us: side_by_side(): lax.all_to_all(both, axis, split_axis=split_dim, concat_axis=concat_dim,...]
    pallas_call x0 -> x3, Pallas kernels: none -> 123 us  [the longest x1 61.9 us: gather_logits(): pl.pallas_call(gather_logits_kernel, out_shape=jax.ShapeDtypeStruct((96,...]
    all_to_all x1 -> x0, blocking collectives: 62.7 us -> none  [sent_to_all(): lax.all_to_all(jnp.broadcast_to(shard[None], (size, *shard.shape)), axis,...]
    reduce_scatter x1 -> x0, waiting for transfers between devices: 55.1 us -> none  [per_device(): lax.psum_scatter(jnp.dot(gathered, head_weight, preferred_element_type=jn...]
    dot_general x6 -> x0, matrix products: 20.8 us -> none  [the longest x1 6.74 us: per_device(): jnp.einsum('sj,src->rjc', tile_match, received, precision=lax.Precision.H...]
    another operation x2 -> x0, local copies, waits for them, and re-layouts: 17.9 us -> none  [the longest x1 9.36 us: per_device(): received = arrived.reshape(vocab_count * CAP, row_count, TILE)]
    all_to_all x2 -> x0, starting transfers between devices: 15.9 us -> none  [the longest x1 10.5 us: sent_to_all(): lax.all_to_all(jnp.broadcast_to(shard[None], (size, *shard.shape)), axis,...]
    concatenate x2 -> x0, other arithmetic: 8.72 us -> none  [the longest x1 8.71 us: side_by_side(): both = jnp.concatenate(columns, axis=along)]
  transfers between devices with their start and end apart: 3 -> 0, of which waited for: 3 -> 0; matrix products, arithmetic and copies ran while one was open for 0% -> 0% of each run, Pallas kernels for 0% -> 0%
where the time goes in v1:
time: 128 us
  Pallas kernels  123 us (96%)
  local copies, waits for them, and re-layouts  4.67 us (4%)
    pallas_call x1, Pallas kernels, gather_logits(): pl.pallas_call(gather_logits_kernel, out_shape=jax.ShapeDtypeStruct((96,...  61.9 us
    pallas_call x1, Pallas kernels, exchange(): pl.pallas_call(exchange_kernel, out_shape=jax.ShapeDtypeStruct((96, width...  53.2 us
    pallas_call x1, Pallas kernels, map_tiles(): pl.pallas_call(map_tiles_kernel, out_shape=(jax.ShapeDtypeStruct((groups...  7.75 us
    unnamed x2, local copies, waits for them, and re-layouts  3.29 us

profile of v1, /device:TPU:1, one launch (start us, length us, event | category | flops | bytes accessed | tf_op | source)
XLA Modules:
  0.0 127.5 jit_solution(15791711357449987473)
XLA Ops:
  0.0 1.4 %pad.4.hid_ref = bf16[16,1024]{1,0:T(8,128)(2,1)} pad(bf16[12,1024]{1,0:T(8,128)(2,1)} %param.4, bf16[]{:T(256)} %constant.2.clone.1), padding=0_4x0_0 | pad | bytes 57346 | tf_op jit(solution)/shard_map/jit(_pad)/pad | solution.py:533
  1.4 1.4 %copy.5.tiles_ref = s32[64,2]{1,0:T(8,128)} copy(s32[64,2]{0,1:T(2,128)} %param.6) | data formatting | bytes 1024 | tf_op args[2]
  2.8 61.9 %gather_logits.1.logits_ref = f32[96,1280]{1,0:T(8,128)} custom-call(bf16[16,1024]{1,0:T(8,128)(2,1)} %pad.4.hid_ref, bf16[1024,1280]{1,0:T(8,128)(2,1)} %w_hbm.1), custom_call_target="tpu_custom_call" | custom-call | tf_op jit(solution)/shard_map/gather_logits/pallas_call | solution.py:216
  64.6 7.7 %map_tiles.1 = (bf16[128,96,128]{2,1,0:T(8,128)(2,1)}, f32[8,32,128]{2,1,0:T(8,128)}) custom-call(s32[64,2]{1,0:T(8,128)} %copy.5.tiles_ref, f32[96,1280]{1,0:T(8,128)} %gather_logits.1.logits_ref, bf16[64,128,128]{2,1,0:T(8,128)(2,1)} %blocks_ref.1), custom_call_target="tpu_custom_call" | custom-call | tf_op jit(solution)/shard_map/map_tiles/pallas_call | solution.py:297
  72.4 53.2 %exchange.1 = f32[96,1536]{1,0:T(8,128)} custom-call(bf16[128,96,128]{2,1,0:T(8,128)(2,1)} %get-tuple-element.7.slots_hbm, f32[8,32,128]{2,1,0:T(8,128)} %get-tuple-element.8.meta_hbm), custom_call_target="tpu_custom_call" | custom-call | tf_op jit(solution)/shard_map/exchange/pallas_call | solution.py:507
  125.6 1.9 %copy.7 = f32[96,1536]{1,0:T(8,128)} copy(f32[96,1536]{1,0:T(8,128)} %exchange.1) | data formatting | bytes 1179648

commit v2 on v0

v2 whole, which is shorter than its diff:
```python
import functools

import jax
import jax.numpy as jnp
from jax import lax
from jax.experimental import pallas as pl
from jax.experimental.pallas import tpu as pltpu
from jax.sharding import PartitionSpec as P

TILE = 128
STILES = 12
CAP = 2
TEACHER_TILES = 10
NX, NY, NC, NZ = 4, 8, 2, 8
MESH = pl.DeviceIdType.MESH
VMEM_LIMIT = 60 * 1024 * 1024
ORDER = (4, 3, -3, 2, -2, 1, -1, 0)
F32, BF16, I16, I32 = jnp.float32, jnp.bfloat16, jnp.int16, jnp.int32
TINY = 1e-30
FULL = 32767.0


def index_of(x, y, c):
    return (x * NY + y) * NC + c


def my_place():
    v = lax.axis_index("vocab")
    return v // (NY * NC), (v // NC) % NY, v % NC


def to_vocab(x, y, c):
    return {"vocab": index_of(x, y, c)}


def signal_all(peers):
    barrier = pltpu.get_barrier_semaphore()
    for peer in peers:
        pl.semaphore_signal(barrier, inc=1, device_id=peer, device_id_type=MESH)
    pl.semaphore_wait(barrier, len(peers))


def remote(src, dst, send_sem, recv_sem, peer):
    return pltpu.make_async_remote_copy(
        src_ref=src, dst_ref=dst, send_sem=send_sem, recv_sem=recv_sem,
        device_id=peer, device_id_type=MESH,
    )


def coded(value):
    top = jnp.maximum(jnp.max(jnp.abs(value), axis=1, keepdims=True), TINY)
    codes = jnp.round(value * (FULL / top)).astype(I32).astype(I16)
    return codes, top * (1.0 / FULL)


def lane_is(shape, lane):
    return lax.broadcasted_iota(I32, shape, 1) == lane


def ring_halves(step, side):
    return ((side,), (1 - side, side), (0, 1), (0, 1))[step]


def plan_kernel(tiles_ref, entry_ref, teacher_ref, valid_ref, label_ref, count_ref):
    first = lax.axis_index("vocab") * TEACHER_TILES
    label_ref[...] = jnp.full(label_ref.shape, -1.0, F32)

    def clear(i, carry):
        entry_ref[i] = 0
        teacher_ref[i] = 0
        valid_ref[i] = 0.0
        return carry

    lax.fori_loop(0, NX * NY * NC * CAP, clear, 0, unroll=8)

    def clear_count(i, carry):
        count_ref[i] = 0
        return carry

    lax.fori_loop(0, NX * NY * NC, clear_count, 0, unroll=8)

    def entry(e, carry):
        student = tiles_ref[e, 1]
        owner = student // STILES
        label = student - owner * STILES
        rank = count_ref[owner]
        count_ref[owner] = rank + 1
        group = (owner // (NY * NC)) * NC + owner % NC
        line = ((owner // NC) % NY) * CAP + rank
        slot = group * (NY * CAP) + line
        entry_ref[slot] = e
        teacher_ref[slot] = tiles_ref[e, 0] - first
        valid_ref[slot] = 1.0
        label_ref[group, pl.ds(line, 1), :] = jnp.full((1, 128), label.astype(F32))
        return carry

    lax.fori_loop(0, tiles_ref.shape[0], entry, 0, unroll=4)


def plan(focus_tiles):
    slots = NX * NY * NC * CAP
    smem = pl.BlockSpec(memory_space=pltpu.SMEM)
    return pl.pallas_call(
        plan_kernel,
        out_shape=(
            jax.ShapeDtypeStruct((slots,), I32),
            jax.ShapeDtypeStruct((slots,), I32),
            jax.ShapeDtypeStruct((slots,), F32),
            jax.ShapeDtypeStruct((NX * NC, NY * CAP, 128), F32),
        ),
        in_specs=[smem],
        out_specs=(smem, smem, smem, pl.BlockSpec(memory_space=pltpu.VMEM)),
        scratch_shapes=[pltpu.SMEM((NX * NY * NC,), I32)],
        name="plan",
    )(focus_tiles)


def whole_kernel(
    entry_ref, teacher_ref, valid_ref, hid_ref, w_hbm, blocks_hbm, label_hbm, out_ref,
    w_ref, blocks_ref, all_ref, part_ref, zout, zin, zout_scale, zin_scale, logits_ref,
    weights_ref, slots_ref, slots_in, label_in, stat_ref, stat_in, factor_ref, group_ref,
    done_ref, yout, yin, yout_stat, yin_stat,
    w_sem, blocks_sem, own_sem, ysend, yrecv, xsend, xrecv, rsend, rrecv, csend, crecv,
    zsend, zrecv, zssend, zsrecv, ssend, srecv, lsend, lrecv, tsend, trecv,
    hsend, hrecv, hssend, hsrecv,
):
    x, y, c = my_place()
    z = lax.axis_index("hid")
    load_w = pltpu.make_async_copy(w_hbm, w_ref, w_sem)
    load_w.start()
    load_blocks = pltpu.make_async_copy(blocks_hbm, blocks_ref, blocks_sem)
    load_blocks.start()
    xs = ((x + 1) % NX, (x + NX - 1) % NX)
    ys = ((y + 1) % NY, (y + NY - 1) % NY)
    zs = ((z + 1) % NZ, (z + NZ - 1) % NZ)

    def place(o):
        return (x + o // 2) % NX, (c + o % 2) % NC

    def place_vocab(o):
        px, pc = place(o)
        return to_vocab(px, y, pc)

    peers = [to_vocab(x, (y + d) % NY, c) for d in range(1, NY)]
    peers += [place_vocab(o) for o in range(1, 8)]
    peers += [{"hid": n} for n in zs]
    signal_all(peers)

    me = index_of(x, y, c)
    sent = []
    arrived = {}

    def send(src, block, send_sem, recv_sem, peer):
        copy = remote(src, all_ref.at[block], send_sem, recv_sem, peer)
        copy.start()
        sent.append(copy)
        return copy

    for d in (4, 3, 5, 2, 6, 1, 7):
        arrived["y", d] = send(
            hid_ref, me, ysend.at[d], yrecv.at[d], to_vocab(x, (y + d) % NY, c)
        )
    own = pltpu.make_async_copy(hid_ref, all_ref.at[me], own_sem)
    own.start()
    for d in (0, 1, 7, 2, 6, 3, 5, 4):
        block = index_of(x, (y + NY - d) % NY, c)
        src = all_ref.at[block]
        if d == 0:
            src = hid_ref
        else:
            arrived["y", d].wait_recv()
        for side in (0, 1):
            arrived["x", side, d] = send(
                src, block, xsend.at[side, d], xrecv.at[side, d], to_vocab(xs[side], y, c)
            )
        arrived["c", 0, d] = send(
            src, block, csend.at[0, d], crecv.at[0, d], to_vocab(x, y, 1 - c)
        )
    for d in (0, 1, 7, 2, 6, 3, 5, 4):
        for side in (0, 1):
            arrived["x", side, d].wait_recv()
            block = index_of(xs[1 - side], (y + NY - d) % NY, c)
            src = all_ref.at[block]
            if d % 2 == side:
                arrived["r", d] = send(
                    src, block, rsend.at[d], rrecv.at[d], to_vocab(xs[side], y, c)
                )
            arrived["c", 1 + side, d] = send(
                src, block, csend.at[1 + side, d], crecv.at[1 + side, d],
                to_vocab(x, y, 1 - c),
            )
    for d in (0, 1, 7, 2, 6, 3, 5, 4):
        arrived["r", d].wait_recv()
        block = index_of((x + 2) % NX, (y + NY - d) % NY, c)
        arrived["c", 3, d] = send(
            all_ref.at[block], block, csend.at[3, d], crecv.at[3, d],
            to_vocab(x, y, 1 - c),
        )
    own.wait()
    load_w.wait()
    for kind in range(4):
        for d in range(NY):
            arrived["c", kind, d].wait_recv()

    came = {}
    for o in range(8):
        px, pc = place(o)
        src = label_hbm.at[px * NC + pc]
        if o == 0:
            copy = pltpu.make_async_copy(src, label_in.at[0], lrecv.at[0])
        else:
            copy = remote(src, label_in.at[o], lsend.at[o], lrecv.at[o], place_vocab(o))
            sent.append(copy)
        copy.start()
        came["l", o] = copy

    def wait_came(key):
        if key[-1] == 0:
            came[key].wait()
        else:
            came[key].wait_recv()

    columns = 256

    def partial(k):
        target = (z + ORDER[k] + NZ) % NZ
        rows = all_ref[pl.ds(target * 8, 8)].reshape(128, all_ref.shape[2])

        def body(n, carry):
            at = pl.ds(pl.multiple_of(n * columns, columns), columns)
            p = jnp.dot(rows, w_ref[:, at], preferred_element_type=F32)
            for i in range(4):
                q = p[32 * i : 32 * i + 32]
                part_ref[k, pl.ds(24 * i, 8), at] = q[0:8]
                part_ref[k, pl.ds(24 * i + 8, 8), at] = q[16:24]
                part_ref[k, pl.ds(24 * i + 16, 8), at] = q[8:16] + pltpu.roll(q[24:32], 4, 0)
            return carry

        lax.fori_loop(0, w_ref.shape[1] // columns, body, 0)

    zhalf = w_ref.shape[1] // 2
    hops = {}

    def send_hop(key, copies):
        for copy in copies:
            copy.start()
            sent.append(copy)
        hops[key] = copies

    def wait_hop(key):
        for copy in hops[key]:
            copy.wait_recv()

    def zvalue(at, g):
        return zin[at + (pl.ds(16 * g, 16),)].astype(F32) * zin_scale[at][:, g : g + 1]

    def zhop(part, side, step, ch, k):
        at = (part, side, step, ch)
        before = (part, side, step - 1, ch)
        has_input = step >= 1 and ch in ring_halves(step - 1, side)
        if has_input:
            wait_hop(("z",) + before)
        scales = jnp.zeros((16, 128), F32)
        for g in range(3):
            value = part_ref[k, pl.ds(48 * part + 16 * g, 16), ch * zhalf : (ch + 1) * zhalf]
            if has_input:
                value = value + zvalue(before, g)
            codes, scale = coded(value)
            zout[at + (pl.ds(16 * g, 16),)] = codes
            scales = jnp.where(lane_is((16, 128), g), scale, scales)
        zout_scale[at] = scales
        peer = {"hid": zs[side]}
        send_hop(("z",) + at, (
            remote(zout_scale.at[at], zin_scale.at[at], zssend.at[at], zsrecv.at[at], peer),
            remote(zout.at[at], zin.at[at], zsend.at[at], zrecv.at[at], peer),
        ))

    def zstep(part, step):
        for turn in (0, 1):
            for side in (0, 1):
                if turn < len(ring_halves(step, side)):
                    k = 0 if step == 0 else 2 * step - 1 + side
                    zhop(part, side, step, ring_halves(step, side)[turn], k)

    def zfinal(part):
        for ch in (0, 1):
            cols = slice(ch * zhalf, (ch + 1) * zhalf)
            for side in (0, 1):
                wait_hop(("z", part, side, 3, ch))
            for g in range(3):
                rows = pl.ds(48 * part + 16 * g, 16)
                logits_ref[rows, cols] = (
                    part_ref[7, rows, cols]
                    + zvalue((part, 0, 3, ch), g)
                    + zvalue((part, 1, 3, ch), g)
                )

    def map_and_send(part):
        stats = jnp.zeros((16, 128), F32)
        for g in range(3):
            logits = logits_ref[pl.ds(48 * part + 16 * g, 16), :]
            top = jnp.max(logits, axis=1, keepdims=True)
            values = jnp.exp(logits - top)
            total = jnp.sum(values, axis=1, keepdims=True)
            for t in range(TEACHER_TILES):
                weights_ref[part, t, pl.ds(16 * g, 16), :] = values[
                    :, t * TILE : (t + 1) * TILE
                ].astype(BF16)
            stats = jnp.where(lane_is((16, 128), g), top, stats)
            stats = jnp.where(lane_is((16, 128), 8 + g), total, stats)
        stat_ref[part] = stats
        for o in range(8):
            src, dst = stat_ref.at[part], stat_in.at[part, o]
            if o == 0:
                copy = pltpu.make_async_copy(src, dst, trecv.at[part, 0])
            else:
                copy = remote(src, dst, tsend.at[part, o], trecv.at[part, o], place_vocab(o))
                sent.append(copy)
            copy.start()
            came["t", part, o] = copy
        for k in range(8):
            row = (y + ORDER[k] + NY) % NY

            def products(o, carry, row=row):
                base = (((x + o // 2) % NX * NC + (c + o % 2) % NC) * NY + row) * CAP
                for i in range(CAP):
                    product = jnp.dot(
                        weights_ref[part, teacher_ref[base + i]],
                        blocks_ref[entry_ref[base + i]],
                        preferred_element_type=F32,
                    )
                    slots_ref[part, base + i] = (product * valid_ref[base + i]).astype(BF16)
                return carry

            lax.fori_loop(0, 8, products, 0, unroll=4)
            for o in (4, 5, 2, 6, 3, 7, 1, 0):
                px, pc = place(o)
                src = slots_ref.at[part, pl.ds(((px * NC + pc) * NY + row) * CAP, CAP)]
                at = (part, k, o)
                if o == 0:
                    copy = pltpu.make_async_copy(src, slots_in.at[at], srecv.at[at])
                else:
                    copy = remote(
                        src, slots_in.at[at], ssend.at[at], srecv.at[at], place_vocab(o)
                    )
                    sent.append(copy)
                copy.start()
                came[("s",) + at] = copy

    def factors(part):
        for o in range(8):
            wait_came(("t", part, o))
        groups = jnp.zeros((16, 128), F32)
        for g in range(3):
            tops = [stat_in[part, o, :, g : g + 1] for o in range(8)]
            top = functools.reduce(jnp.maximum, tops)
            total = jnp.zeros((16, 1), F32)
            for o in range(8):
                factor = jnp.exp(tops[o] - top)
                total = total + factor * stat_in[part, o, :, 8 + g : 9 + g]
                factor_ref[part, o, pl.ds(16 * g, 16), :] = jnp.broadcast_to(factor, (16, 128))
            groups = jnp.where(lane_is((16, 128), g), top, groups)
            groups = jnp.where(lane_is((16, 128), 8 + g), total, groups)
        group_ref[part] = groups

    half_tiles = STILES // 2

    def merged(part, k, g, ch):
        row = (y + ORDER[k] + NY) % NY
        at = pl.ds(16 * g, 16)
        tiles = [jnp.zeros((16, TILE), F32)] * half_tiles
        for o in range(8):
            factor = factor_ref[part, o, at, :]
            for i in range(CAP):
                tile = slots_in[part, k, o, i, at, :].astype(F32) * factor
                label = label_in[o, pl.ds(row * CAP + i, 1), :]
                for j in range(half_tiles):
                    mine = label == float(ch * half_tiles + j)
                    tiles[j] = tiles[j] + jnp.where(mine, tile, 0.0)
        group = group_ref[part]
        return tiles, group[:, g : g + 1], group[:, 8 + g : 9 + g]

    def incoming(at, g):
        stat = yin_stat[at]
        return stat[:, g : g + 1], stat[:, 8 + g : 9 + g], stat[:, 16 + g : 17 + g]

    def yhop(part, side, step, ch, k):
        at = (part, side, step, ch)
        before = (part, side, step - 1, ch)
        has_input = step >= 1 and ch in ring_halves(step - 1, side)
        if has_input:
            wait_hop(("y",) + before)
        stats = jnp.zeros((16, 128), F32)
        for g in range(3):
            tiles, top, total = merged(part, k, g, ch)
            if has_input:
                scale, in_top, in_total = incoming(before, g)
                new_top = jnp.maximum(top, in_top)
                mine = jnp.exp(top - new_top)
                theirs = jnp.exp(in_top - new_top)
                total = total * mine + in_total * theirs
                scale = scale * theirs
                top = new_top
                for j in range(half_tiles):
                    code = yin[before + (pl.ds(16 * g, 16), pl.ds(j * TILE, TILE))]
                    tiles[j] = tiles[j] * mine + code.astype(F32) * scale
            codes, scale = coded(jnp.concatenate(tiles, axis=1))
            yout[at + (pl.ds(16 * g, 16),)] = codes
            stats = jnp.where(lane_is((16, 128), g), scale, stats)
            stats = jnp.where(lane_is((16, 128), 8 + g), top, stats)
            stats = jnp.where(lane_is((16, 128), 16 + g), total, stats)
        yout_stat[at] = stats
        peer = to_vocab(x, ys[side], c)
        send_hop(("y",) + at, (
            remote(yout_stat.at[at], yin_stat.at[at], hssend.at[at], hsrecv.at[at], peer),
            remote(yout.at[at], yin.at[at], hsend.at[at], hrecv.at[at], peer),
        ))

    def wait_stage(part, k):
        for o in range(8):
            wait_came(("s", part, k, o))

    def ystep(part, step):
        for side in (0, 1):
            k = 0 if step == 0 else 2 * step - 1 + side
            if step > 0 or side == 0:
                wait_stage(part, k)
            for ch in ring_halves(step, side):
                yhop(part, side, step, ch, k)

    def yfinal(part):
        wait_stage(part, 7)
        for ch in (0, 1):
            for side in (0, 1):
                wait_hop(("y", part, side, 3, ch))
            for g in range(3):
                tiles, top, total = merged(part, 7, g, ch)
                parts = [incoming((part, side, 3, ch), g) for side in (0, 1)]
                new_top = jnp.maximum(top, jnp.maximum(parts[0][1], parts[1][1]))
                mine = jnp.exp(top - new_top)
                theirs = [jnp.exp(p[1] - new_top) for p in parts]
                total = total * mine + parts[0][2] * theirs[0] + parts[1][2] * theirs[1]
                share = float(STILES * TILE * NX * NY * NC) / total
                for j in range(half_tiles):
                    value = tiles[j] * mine
                    for side in (0, 1):
                        code = yin[part, side, 3, ch, pl.ds(16 * g, 16), pl.ds(j * TILE, TILE)]
                        value = value + code.astype(F32) * (parts[side][0] * theirs[side])
                    at = (ch * half_tiles + j) * TILE
                    done_ref[pl.ds(48 * part + 16 * g, 16), pl.ds(at, TILE)] = value * share
        early = lax.broadcasted_iota(I32, (8, done_ref.shape[1]), 0) < 4
        for p in (2 * part, 2 * part + 1):
            second = pltpu.roll(done_ref[24 * p + 8 : 24 * p + 16, :], 4, 0)
            mixed = done_ref[24 * p + 16 : 24 * p + 24, :]
            out_ref[24 * p : 24 * p + 8, :] = done_ref[24 * p : 24 * p + 8, :]
            out_ref[24 * p + 8 : 24 * p + 16, :] = jnp.where(early, mixed, second)
            out_ref[24 * p + 16 : 24 * p + 24, :] = jnp.where(early, second, mixed)

    partial(0)
    zstep(0, 0)
    partial(1)
    partial(2)
    zstep(0, 1)
    zstep(1, 0)
    partial(3)
    partial(4)
    zstep(0, 2)
    zstep(1, 1)
    partial(5)
    partial(6)
    zstep(0, 3)
    zstep(1, 2)
    partial(7)
    load_blocks.wait()
    zfinal(0)
    map_and_send(0)
    zstep(1, 3)
    zfinal(1)
    map_and_send(1)
    for o in range(8):
        wait_came(("l", o))
    for part in (0, 1):
        factors(part)
        for step in range(4):
            ystep(part, step)
        yfinal(part)
    for copy in sent:
        copy.wait_send()


def whole(entry, teacher, valid, hidden, head_weight, blocks, labels):
    depth, width = head_weight.shape
    student = STILES * TILE
    dma = pltpu.SemaphoreType.DMA
    smem = pl.BlockSpec(memory_space=pltpu.SMEM)
    vmem = pl.BlockSpec(memory_space=pltpu.VMEM)
    anywhere = pl.BlockSpec(memory_space=pl.ANY)
    ring = (2, 2, 4, 2)
    return pl.pallas_call(
        whole_kernel,
        out_shape=jax.ShapeDtypeStruct((96, student), F32),
        in_specs=[smem, smem, smem, vmem, anywhere, anywhere, anywhere],
        out_specs=vmem,
        scratch_shapes=[
            pltpu.VMEM((depth, width), BF16),
            pltpu.VMEM(blocks.shape, BF16),
            pltpu.VMEM((NX * NY * NC, 16, depth), BF16),
            pltpu.VMEM((8, 96, width), F32),
            pltpu.VMEM(ring + (48, width // 2), I16),
            pltpu.VMEM(ring + (48, width // 2), I16),
            pltpu.VMEM(ring + (16, 128), F32),
            pltpu.VMEM(ring + (16, 128), F32),
            pltpu.VMEM((96, width), F32),
            pltpu.VMEM((2, TEACHER_TILES, 48, TILE), BF16),
            pltpu.VMEM((2, NX * NY * NC * CAP, 48, TILE), BF16),
            pltpu.VMEM((2, 8, 8, CAP, 48, TILE), BF16),
            pltpu.VMEM((8, NY * CAP, 128), F32),
            pltpu.VMEM((2, 16, 128), F32),
            pltpu.VMEM((2, 8, 16, 128), F32),
            pltpu.VMEM((2, 8, 48, TILE), F32),
            pltpu.VMEM((2, 16, 128), F32),
            pltpu.VMEM((96, student), F32),
            pltpu.VMEM(ring + (48, student // 2), I16),
            pltpu.VMEM(ring + (48, student // 2), I16),
            pltpu.VMEM(ring + (16, 128), F32),
            pltpu.VMEM(ring + (16, 128), F32),
            dma, dma, dma, dma((NY,)), dma((NY,)), dma((2, NY)), dma((2, NY)),
            dma((NY,)), dma((NY,)), dma((4, NY)), dma((4, NY)),
            dma(ring), dma(ring), dma(ring), dma(ring),
            dma((2, 8, 8)), dma((2, 8, 8)), dma((8,)), dma((8,)), dma((2, 8)), dma((2, 8)),
            dma(ring), dma(ring), dma(ring), dma(ring),
        ],
        compiler_params=pltpu.CompilerParams(
            collective_id=0, has_side_effects=True, vmem_limit_bytes=VMEM_LIMIT
        ),
        name="whole",
    )(entry, teacher, valid, hidden, head_weight, blocks, labels)


def per_device(hidden_states, head_weight, focus_tiles, focus_blocks):
    hidden = jnp.pad(hidden_states, ((0, 16 - hidden_states.shape[0]), (0, 0)))
    entry, teacher, valid, labels = plan(focus_tiles)
    return whole(entry, teacher, valid, hidden, head_weight, focus_blocks, labels)


def solution(mesh):
    return jax.shard_map(
        per_device,
        mesh=mesh,
        in_specs=(P("vocab", "hid"), P("hid", "vocab"), P("vocab", None), P("vocab", None, None)),
        out_specs=P("hid", "vocab"),
        check_vma=False,
    )
```

time: 373 us -> 131 us (0.35)
  the two profiles are of different devices: /device:TPU:1 before, /device:TPU:16 now
where the time goes in v2:
time: 131 us; the launch traced here: 130 us
  Pallas kernels  125 us (95%)
  local copies, waits for them, and re-layouts  4.68 us (4%)
    pallas_call x1, Pallas kernels, whole(): pl.pallas_call(whole_kernel, out_shape=jax.ShapeDtypeStruct((96, student)...  122 us
    pallas_call x1, Pallas kernels, plan(): pl.pallas_call(plan_kernel, out_shape=(jax.ShapeDtypeStruct((slots,), I32...  3.74 us
    unnamed x2, local copies, waits for them, and re-layouts  3.3 us

profile of v2, /device:TPU:16, one launch (start us, length us, event | category | flops | bytes accessed | tf_op | source)
XLA Modules:
  0.0 130.1 jit_solution(18056214746489814262)
XLA Ops:
  0.0 1.4 %pad.4.hid_ref = bf16[16,1024]{1,0:T(8,128)(2,1)} pad(bf16[12,1024]{1,0:T(8,128)(2,1)} %param.4, bf16[]{:T(256)} %constant.2.clone.1), padding=0_4x0_0 | pad | bytes 57346 | tf_op jit(solution)/shard_map/jit(_pad)/pad | solution.py:541
  1.4 1.4 %copy.5.tiles_ref = s32[64,2]{1,0:T(8,128)} copy(s32[64,2]{0,1:T(2,128)} %param.6) | data formatting | bytes 1024 | tf_op args[2]
  2.8 3.7 %plan.1 = (s32[128]{0:T(128)}, s32[128]{0:T(128)}, f32[128]{0:T(128)}, f32[8,16,128]{2,1,0:T(8,128)}) custom-call(s32[64,2]{1,0:T(8,128)} %copy.5.tiles_ref), custom_call_target="tpu_custom_call" | custom-call | tf_op jit(solution)/shard_map/plan/pallas_call | solution.py:103
  6.5 121.7 %whole.1 = f32[96,1536]{1,0:T(8,128)} custom-call(s32[128]{0:T(128)} %get-tuple-element.9.entry_ref, s32[128]{0:T(128)} %get-tuple-element.10.teacher_ref, f32[128]{0:T(128)} %get-tuple-element.11.valid_ref, bf16[16,1024]{1,0:T(8,128)(2,1)} %pad.4.hid_ref, bf16[1024,1280]{1,0:T(8,128)(2,1)} %w_hbm.1, bf16[64,128,128]{2,1,0:T(8,128)(2,1)} %blocks_hbm.1, ...), custom_call_target="tpu_custom_call" | custom-call | tf_op jit(solution)/shard_map/whole/pallas_call | solution.py:499
  128.2 1.9 %copy.7 = f32[96,1536]{1,0:T(8,128)} copy(f32[96,1536]{1,0:T(8,128)} %whole.1) | data formatting | bytes 1179648

commit v3 on v2

--- a/solution.py
+++ b/solution.py
@@ -61,14 +61,18 @@
     return ((side,), (1 - side, side), (0, 1), (0, 1))[step]
 
 
-def plan_kernel(tiles_ref, entry_ref, teacher_ref, valid_ref, label_ref, count_ref):
+def plan_kernel(tiles_ref, hid_ref, entry_ref, teacher_ref, label_ref, padded_ref, count_ref):
     first = lax.axis_index("vocab") * TEACHER_TILES
+    rows, depth = hid_ref.shape
+    padded_ref[...] = jnp.concatenate(
+        [hid_ref[...].astype(F32), jnp.zeros((16 - rows, depth), F32)], axis=0
+    ).astype(BF16)
     label_ref[...] = jnp.full(label_ref.shape, -1.0, F32)
+    slot_of_lane = (lax.broadcasted_iota(I32, (1, 128), 1) // 16) % CAP
 
     def clear(i, carry):
         entry_ref[i] = 0
-        teacher_ref[i] = 0
-        valid_ref[i] = 0.0
+        teacher_ref[i] = TEACHER_TILES
         return carry
 
     lax.fori_loop(0, NX * NY * NC * CAP, clear, 0, unroll=8)
@@ -80,48 +84,51 @@
     lax.fori_loop(0, NX * NY * NC, clear_count, 0, unroll=8)
 
     def entry(e, carry):
-        student = tiles_ref[e, 1]
+        student = tiles_ref[1, e]
         owner = student // STILES
         label = student - owner * STILES
         rank = count_ref[owner]
         count_ref[owner] = rank + 1
         group = (owner // (NY * NC)) * NC + owner % NC
-        line = ((owner // NC) % NY) * CAP + rank
-        slot = group * (NY * CAP) + line
+        row = (owner // NC) % NY
+        slot = (group * NY + row) * CAP + rank
         entry_ref[slot] = e
-        teacher_ref[slot] = tiles_ref[e, 0] - first
-        valid_ref[slot] = 1.0
-        label_ref[group, pl.ds(line, 1), :] = jnp.full((1, 128), label.astype(F32))
+        teacher_ref[slot] = tiles_ref[0, e] - first
+        line = label_ref[group, pl.ds(row, 1), :]
+        label_ref[group, pl.ds(row, 1), :] = jnp.where(
+            slot_of_lane == rank, label.astype(F32), line
+        )
         return carry
 
-    lax.fori_loop(0, tiles_ref.shape[0], entry, 0, unroll=4)
-
-
-def plan(focus_tiles):
+    lax.fori_loop(0, tiles_ref.shape[1], entry, 0, unroll=4)
+
+
+def plan(focus_tiles, hidden):
     slots = NX * NY * NC * CAP
     smem = pl.BlockSpec(memory_space=pltpu.SMEM)
+    vmem = pl.BlockSpec(memory_space=pltpu.VMEM)
     return pl.pallas_call(
         plan_kernel,
         out_shape=(
             jax.ShapeDtypeStruct((slots,), I32),
             jax.ShapeDtypeStruct((slots,), I32),
-            jax.ShapeDtypeStruct((slots,), F32),
-            jax.ShapeDtypeStruct((NX * NC, NY * CAP, 128), F32),
+            jax.ShapeDtypeStruct((NX * NC, NY, 128), F32),
+            jax.ShapeDtypeStruct((16, hidden.shape[1]), BF16),
         ),
-        in_specs=[smem],
-        out_specs=(smem, smem, smem, pl.BlockSpec(memory_space=pltpu.VMEM)),
+        in_specs=[smem, vmem],
+        out_specs=(smem, smem, vmem, vmem),
         scratch_shapes=[pltpu.SMEM((NX * NY * NC,), I32)],
         name="plan",
-    )(focus_tiles)
+    )(focus_tiles.T, hidden)
 
 
 def whole_kernel(
-    entry_ref, teacher_ref, valid_ref, hid_ref, w_hbm, blocks_hbm, label_hbm, out_ref,
+    entry_ref, teacher_ref, hid_ref, w_hbm, blocks_hbm, label_hbm, out_ref,
     w_ref, blocks_ref, all_ref, part_ref, zout, zin, zout_scale, zin_scale, logits_ref,
-    weights_ref, slots_ref, slots_in, label_in, stat_ref, stat_in, factor_ref, group_ref,
-    done_ref, yout, yin, yout_stat, yin_stat,
+    weights_ref, slots_ref, slots_in, label_in, top_ref, top_in, total_ref, total_in, group_ref,
+    pick_ref, merged_ref, done_ref, yout, yin, yout_stat, yin_stat,
     w_sem, blocks_sem, own_sem, ysend, yrecv, xsend, xrecv, rsend, rrecv, csend, crecv,
-    zsend, zrecv, zssend, zsrecv, ssend, srecv, lsend, lrecv, tsend, trecv,
+    zsend, zrecv, zssend, zsrecv, ssend, srecv, lsend, lrecv, tsend, trecv, usend, urecv,
     hsend, hrecv, hssend, hsrecv,
 ):
     x, y, c = my_place()
@@ -295,29 +302,44 @@
                     + zvalue((part, 1, 3, ch), g)
                 )
 
+    def to_group(name, part, src, into, send_sem, recv_sem):
+        for o in range(8):
+            dst = into.at[part, o]
+            if o == 0:
+                copy = pltpu.make_async_copy(src, dst, recv_sem.at[part, 0])
+            else:
+                copy = remote(
+                    src, dst, send_sem.at[part, o], recv_sem.at[part, o], place_vocab(o)
+                )
+                sent.append(copy)
+            copy.start()
+            came[name, part, o] = copy
+
+    def send_tops(part):
+        tops = jnp.zeros((16, 128), F32)
+        for g in range(3):
+            top = jnp.max(logits_ref[pl.ds(48 * part + 16 * g, 16), :], axis=1, keepdims=True)
+            tops = jnp.where(lane_is((16, 128), g), top, tops)
+        top_ref[part] = tops
+        to_group("top", part, top_ref.at[part], top_in, tsend, trecv)
+
     def map_and_send(part):
-        stats = jnp.zeros((16, 128), F32)
+        for o in range(8):
+            wait_came(("top", part, o))
+        tops = functools.reduce(jnp.maximum, [top_in[part, o] for o in range(8)])
+        totals = jnp.zeros((16, 128), F32)
+        weights_ref[part, TEACHER_TILES] = jnp.zeros((48, TILE), BF16)
         for g in range(3):
             logits = logits_ref[pl.ds(48 * part + 16 * g, 16), :]
-            top = jnp.max(logits, axis=1, keepdims=True)
-            values = jnp.exp(logits - top)
+            values = jnp.exp(logits - tops[:, g : g + 1])
             total = jnp.sum(values, axis=1, keepdims=True)
             for t in range(TEACHER_TILES):
                 weights_ref[part, t, pl.ds(16 * g, 16), :] = values[
                     :, t * TILE : (t + 1) * TILE
                 ].astype(BF16)
-            stats = jnp.where(lane_is((16, 128), g), top, stats)
-            stats = jnp.where(lane_is((16, 128), 8 + g), total, stats)
-        stat_ref[part] = stats
-        for o in range(8):
-            src, dst = stat_ref.at[part], stat_in.at[part, o]
-            if o == 0:
-                copy = pltpu.make_async_copy(src, dst, trecv.at[part, 0])
-            else:
-                copy = remote(src, dst, tsend.at[part, o], trecv.at[part, o], place_vocab(o))
-                sent.append(copy)
-            copy.start()
-            came["t", part, o] = copy
+            totals = jnp.where(lane_is((16, 128), 8 + g), total, totals)
+        total_ref[part] = totals
+        to_group("total", part, total_ref.at[part], total_in, usend, urecv)
         for k in range(8):
             row = (y + ORDER[k] + NY) % NY
 
@@ -329,7 +351,7 @@
                         blocks_ref[entry_ref[base + i]],
                         preferred_element_type=F32,
                     )
-                    slots_ref[part, base + i] = (product * valid_ref[base + i]).astype(BF16)
+                    slots_ref[part, base + i] = product.astype(BF16)
                 return carry
 
             lax.fori_loop(0, 8, products, 0, unroll=4)
@@ -347,37 +369,47 @@
                 copy.start()
                 came[("s",) + at] = copy
 
-    def factors(part):
+    def group_stats(part):
         for o in range(8):
-            wait_came(("t", part, o))
-        groups = jnp.zeros((16, 128), F32)
+            wait_came(("total", part, o))
+        tops = functools.reduce(jnp.maximum, [top_in[part, o] for o in range(8)])
+        totals = functools.reduce(jnp.add, [total_in[part, o] for o in range(8)])
+        lanes = lax.broadcasted_iota(I32, (16, 128), 1)
+        group_ref[part] = jnp.where(lanes < 8, tops, totals)
+
+    def pick(k):
+        row = (y + ORDER[k] + NY) % NY
+        shape = (STILES * 16, 128)
+        lines = lax.broadcasted_iota(I32, shape, 0)
+        lanes = lax.broadcasted_iota(I32, shape, 1)
+        tile = (lines // 16).astype(F32)
+        same_position = lines % 16 == lanes % 16
+        quarter = lax.broadcasted_iota(I32, (1, 128), 1) // 32
+        for side in (0, 1):
+            labels = label_in[4 * side, pl.ds(row, 1), :]
+            for q in range(1, 4):
+                labels = jnp.where(quarter == q, label_in[4 * side + q, pl.ds(row, 1), :], labels)
+            chosen = jnp.logical_and(same_position, tile == labels)
+            pick_ref[k, :, 128 * side : 128 * (side + 1)] = jnp.where(
+                chosen, 1.0, 0.0
+            ).astype(BF16)
+
+    def merge(part, k):
+        for o in range(8):
+            wait_came(("s", part, k, o))
         for g in range(3):
-            tops = [stat_in[part, o, :, g : g + 1] for o in range(8)]
-            top = functools.reduce(jnp.maximum, tops)
-            total = jnp.zeros((16, 1), F32)
-            for o in range(8):
-                factor = jnp.exp(tops[o] - top)
-                total = total + factor * stat_in[part, o, :, 8 + g : 9 + g]
-                factor_ref[part, o, pl.ds(16 * g, 16), :] = jnp.broadcast_to(factor, (16, 128))
-            groups = jnp.where(lane_is((16, 128), g), top, groups)
-            groups = jnp.where(lane_is((16, 128), 8 + g), total, groups)
-        group_ref[part] = groups
-
-    half_tiles = STILES // 2
+            slots = slots_in[part, k, :, :, pl.ds(16 * g, 16), :].reshape(16 * 16, TILE)
+            tiles = jnp.dot(pick_ref[k], slots, preferred_element_type=F32)
+            for j in range(STILES):
+                merged_ref[part, k, pl.ds(16 * g, 16), pl.ds(j * TILE, TILE)] = tiles[
+                    16 * j : 16 * (j + 1)
+                ]
+
+    yhalf = STILES * TILE // 2
 
     def merged(part, k, g, ch):
-        row = (y + ORDER[k] + NY) % NY
-        at = pl.ds(16 * g, 16)
-        tiles = [jnp.zeros((16, TILE), F32)] * half_tiles
-        for o in range(8):
-            factor = factor_ref[part, o, at, :]
-            for i in range(CAP):
-                tile = slots_in[part, k, o, i, at, :].astype(F32) * factor
-                label = label_in[o, pl.ds(row * CAP + i, 1), :]
-                for j in range(half_tiles):
-                    mine = label == float(ch * half_tiles + j)
-                    tiles[j] = tiles[j] + jnp.where(mine, tile, 0.0)
         group = group_ref[part]
+        tiles = merged_ref[part, k, pl.ds(16 * g, 16), pl.ds(ch * yhalf, yhalf)]
         return tiles, group[:, g : g + 1], group[:, 8 + g : 9 + g]
 
     def incoming(at, g):
@@ -401,10 +433,9 @@
                 total = total * mine + in_total * theirs
                 scale = scale * theirs
                 top = new_top
-                for j in range(half_tiles):
-                    code = yin[before + (pl.ds(16 * g, 16), pl.ds(j * TILE, TILE))]
-                    tiles[j] = tiles[j] * mine + code.astype(F32) * scale
-            codes, scale = coded(jnp.concatenate(tiles, axis=1))
+                code = yin[before + (pl.ds(16 * g, 16),)]
+                tiles = tiles * mine + code.astype(F32) * scale
+            codes, scale = coded(tiles)
             yout[at + (pl.ds(16 * g, 16),)] = codes
             stats = jnp.where(lane_is((16, 128), g), scale, stats)
             stats = jnp.where(lane_is((16, 128), 8 + g), top, stats)
@@ -416,20 +447,16 @@
             remote(yout.at[at], yin.at[at], hsend.at[at], hrecv.at[at], peer),
         ))
 
-    def wait_stage(part, k):
-        for o in range(8):
-            wait_came(("s", part, k, o))
-
     def ystep(part, step):
         for side in (0, 1):
             k = 0 if step == 0 else 2 * step - 1 + side
             if step > 0 or side == 0:
-                wait_stage(part, k)
+                merge(part, k)
             for ch in ring_halves(step, side):
                 yhop(part, side, step, ch, k)
 
     def yfinal(part):
-        wait_stage(part, 7)
+        merge(part, 7)
         for ch in (0, 1):
             for side in (0, 1):
                 wait_hop(("y", part, side, 3, ch))
@@ -441,13 +468,11 @@
                 theirs = [jnp.exp(p[1] - new_top) for p in parts]
                 total = total * mine + parts[0][2] * theirs[0] + parts[1][2] * theirs[1]
                 share = float(STILES * TILE * NX * NY * NC) / total
-                for j in range(half_tiles):
-                    value = tiles[j] * mine
-                    for side in (0, 1):
-                        code = yin[part, side, 3, ch, pl.ds(16 * g, 16), pl.ds(j * TILE, TILE)]
-                        value = value + code.astype(F32) * (parts[side][0] * theirs[side])
-                    at = (ch * half_tiles + j) * TILE
-                    done_ref[pl.ds(48 * part + 16 * g, 16), pl.ds(at, TILE)] = value * share
+                value = tiles * mine
+                for side in (0, 1):
+                    code = yin[part, side, 3, ch, pl.ds(16 * g, 16), :]
+                    value = value + code.astype(F32) * (parts[side][0] * theirs[side])
+                done_ref[pl.ds(48 * part + 16 * g, 16), pl.ds(ch * yhalf, yhalf)] = value * share
         early = lax.broadcasted_iota(I32, (8, done_ref.shape[1]), 0) < 4
         for p in (2 * part, 2 * part + 1):
             second = pltpu.roll(done_ref[24 * p + 8 : 24 * p + 16, :], 4, 0)
@@ -469,26 +494,35 @@
     partial(5)
     partial(6)
     zstep(0, 3)
-    zstep(1, 2)
     partial(7)
     load_blocks.wait()
     zfinal(0)
+    send_tops(0)
+    zstep(1, 2)
     map_and_send(0)
     zstep(1, 3)
-    zfinal(1)
-    map_and_send(1)
     for o in range(8):
         wait_came(("l", o))
-    for part in (0, 1):
-        factors(part)
-        for step in range(4):
-            ystep(part, step)
-        yfinal(part)
+    for k in range(8):
+        pick(k)
+    zfinal(1)
+    send_tops(1)
+    group_stats(0)
+    ystep(0, 0)
+    map_and_send(1)
+    for step in range(1, 4):
+        ystep(0, step)
+    group_stats(1)
+    ystep(1, 0)
+    yfinal(0)
+    for step in range(1, 4):
+        ystep(1, step)
+    yfinal(1)
     for copy in sent:
         copy.wait_send()
 
 
-def whole(entry, teacher, valid, hidden, head_weight, blocks, labels):
+def whole(entry, teacher, hidden, head_weight, blocks, labels):
     depth, width = head_weight.shape
     student = STILES * TILE
     dma = pltpu.SemaphoreType.DMA
@@ -499,7 +533,7 @@
     return pl.pallas_call(
         whole_kernel,
         out_shape=jax.ShapeDtypeStruct((96, student), F32),
-        in_specs=[smem, smem, smem, vmem, anywhere, anywhere, anywhere],
+        in_specs=[smem, smem, vmem, anywhere, anywhere, anywhere],
         out_specs=vmem,
         scratch_shapes=[
             pltpu.VMEM((depth, width), BF16),
@@ -511,14 +545,17 @@
             pltpu.VMEM(ring + (16, 128), F32),
             pltpu.VMEM(ring + (16, 128), F32),
             pltpu.VMEM((96, width), F32),
-            pltpu.VMEM((2, TEACHER_TILES, 48, TILE), BF16),
+            pltpu.VMEM((2, TEACHER_TILES + 1, 48, TILE), BF16),
             pltpu.VMEM((2, NX * NY * NC * CAP, 48, TILE), BF16),
             pltpu.VMEM((2, 8, 8, CAP, 48, TILE), BF16),
-            pltpu.VMEM((8, NY * CAP, 128), F32),
+            pltpu.VMEM((8, NY, 128), F32),
             pltpu.VMEM((2, 16, 128), F32),
             pltpu.VMEM((2, 8, 16, 128), F32),
-            pltpu.VMEM((2, 8, 48, TILE), F32),
             pltpu.VMEM((2, 16, 128), F32),
+            pltpu.VMEM((2, 8, 16, 128), F32),
+            pltpu.VMEM((2, 16, 128), F32),
+            pltpu.VMEM((8, STILES * 16, 256), BF16),
+            pltpu.VMEM((2, 8, 48, student), F32),
             pltpu.VMEM((96, student), F32),
             pltpu.VMEM(ring + (48, student // 2), I16),
             pltpu.VMEM(ring + (48, student // 2), I16),
@@ -528,19 +565,19 @@
             dma((NY,)), dma((NY,)), dma((4, NY)), dma((4, NY)),
             dma(ring), dma(ring), dma(ring), dma(ring),
             dma((2, 8, 8)), dma((2, 8, 8)), dma((8,)), dma((8,)), dma((2, 8)), dma((2, 8)),
+            dma((2, 8)), dma((2, 8)),
             dma(ring), dma(ring), dma(ring), dma(ring),
         ],
         compiler_params=pltpu.CompilerParams(
             collective_id=0, has_side_effects=True, vmem_limit_bytes=VMEM_LIMIT
         ),
         name="whole",
-    )(entry, teacher, valid, hidden, head_weight, blocks, labels)
+    )(entry, teacher, hidden, head_weight, blocks, labels)
 
 
 def per_device(hidden_states, head_weight, focus_tiles, focus_blocks):
-    hidden = jnp.pad(hidden_states, ((0, 16 - hidden_states.shape[0]), (0, 0)))
-    entry, teacher, valid, labels = plan(focus_tiles)
-    return whole(entry, teacher, valid, hidden, head_weight, focus_blocks, labels)
+    entry, teacher, labels, hidden = plan(focus_tiles, hidden_states)
+    return whole(entry, teacher, hidden, head_weight, focus_blocks, labels)
 
 
 def solution(mesh):

time: 131 us -> 133 us (1.015)
  the two profiles are of different devices: /device:TPU:16 before, /device:TPU:1 now
where the time goes in v3:
time: 133 us; the launch traced here: 130 us
  Pallas kernels  128 us (96%)
  local copies, waits for them, and re-layouts  1.92 us (1%)
    pallas_call x1, Pallas kernels, whole(): pl.pallas_call(whole_kernel, out_shape=jax.ShapeDtypeStruct((96, student)...  125 us
    pallas_call x1, Pallas kernels, plan(): pl.pallas_call(plan_kernel, out_shape=(jax.ShapeDtypeStruct((slots,), I32...  3.2 us

profile of v3, /device:TPU:1, one launch (start us, length us, event | category | flops | bytes accessed | tf_op | source)
XLA Modules:
  0.0 130.2 jit_solution(345650122912392595)
XLA Ops:
  0.0 3.2 %plan.1 = (s32[128]{0:T(128)}, s32[128]{0:T(128)}, f32[8,8,128]{2,1,0:T(8,128)}, bf16[16,1024]{1,0:T(8,128)(2,1)}) custom-call(s32[2,64]{1,0:T(2,128)} %bitcast.1, bf16[12,1024]{1,0:T(8,128)(2,1)} %hid_ref.1), custom_call_target="tpu_custom_call" | custom-call | tf_op jit(solution)/shard_map/plan/pallas_call | solution.py:110
  3.2 125.0 %whole.1 = f32[96,1536]{1,0:T(8,128)} custom-call(s32[128]{0:T(128)} %get-tuple-element.9.entry_ref, s32[128]{0:T(128)} %get-tuple-element.10.teacher_ref, bf16[16,1024]{1,0:T(8,128)(2,1)} %get-tuple-element.11.hid_ref, bf16[1024,1280]{1,0:T(8,128)(2,1)} %w_hbm.1, bf16[64,128,128]{2,1,0:T(8,128)(2,1)} %blocks_hbm.1, f32[8,8,128]{2,1,0:T(8,128)} %get-tuple-element.12.label_hbm), custom_call_target="tpu_custom_call" | custom-call | tf_op jit(solution)/shard_map/whole/pallas_call | solution.py:533
  128.2 1.9 %copy.6 = f32[96,1536]{1,0:T(8,128)} copy(f32[96,1536]{1,0:T(8,128)} %whole.1) | data formatting | bytes 1179648

commit v4 on v1

--- a/solution.py
+++ b/solution.py
@@ -63,7 +63,7 @@
 
 
 def gather_logits_kernel(
-    hid_ref, w_hbm, out_ref, w_ref, all_ref, part_ref,
+    rows_ref, w_hbm, out_ref, hid_ref, w_ref, all_ref, part_ref,
     out_code, in_code, out_scale, in_scale,
     w_sem, own_sem, ysend, yrecv, xsend, xrecv, rsend, rrecv, csend, crecv,
     zsend, zrecv, zssend, zsrecv,
@@ -72,6 +72,10 @@
     z = lax.axis_index("hid")
     load_w = pltpu.make_async_copy(w_hbm, w_ref, w_sem)
     load_w.start()
+    count, depth = rows_ref.shape
+    hid_ref[...] = jnp.concatenate(
+        [rows_ref[...].astype(F32), jnp.zeros((16 - count, depth), F32)], axis=0
+    ).astype(BF16)
     xs = ((x + 1) % NX, (x + NX - 1) % NX)
     zs = ((z + 1) % NZ, (z + NZ - 1) % NZ)
     peers = [to_vocab(x, (y + d) % NY, c) for d in range(1, NY)]
@@ -192,8 +196,9 @@
     for step in range(4):
         for half in (0, 1):
             for side in (0, 1):
-                if half in ring_halves(step, side):
-                    hop(side, step, half, 0 if step == 0 else 2 * step - 1 + side)
+                now = half if step != 1 else (half + 1 - side) % 2
+                if now in ring_halves(step, side):
+                    hop(side, step, now, 0 if step == 0 else 2 * step - 1 + side)
         if step < 3:
             partial(2 * step + 1)
             partial(2 * step + 2)
@@ -222,6 +227,7 @@
         ],
         out_specs=pl.BlockSpec(memory_space=pltpu.VMEM),
         scratch_shapes=[
+            pltpu.VMEM((16, depth), BF16),
             pltpu.VMEM((depth, width), BF16),
             pltpu.VMEM((NX * NY * NC, 16, depth), BF16),
             pltpu.VMEM((8, 96, width), F32),
@@ -266,16 +272,16 @@
         slots_ref[i] = jnp.zeros((96, TILE), BF16)
         return carry
 
-    lax.fori_loop(0, slots_ref.shape[0], clear, 0)
+    lax.fori_loop(0, slots_ref.shape[0], clear, 0, unroll=8)
 
     def clear_count(i, carry):
         count_ref[i] = 0
         return carry
 
-    lax.fori_loop(0, count_ref.shape[0], clear_count, 0)
+    lax.fori_loop(0, count_ref.shape[0], clear_count, 0, unroll=8)
 
     def entry(e, carry):
-        student = tiles_ref[e, 1]
+        student = tiles_ref[1, e]
         owner = student // STILES
         label = student - owner * STILES
         rank = count_ref[owner]
@@ -283,13 +289,13 @@
         group = (owner // (NY * NC)) * NC + owner % NC
         line = ((owner // NC) % NY) * CAP + rank
         product = jnp.dot(
-            weights_ref[tiles_ref[e, 0] - first], blocks_ref[e], preferred_element_type=F32
+            weights_ref[tiles_ref[0, e] - first], blocks_ref[e], preferred_element_type=F32
         )
         slots_ref[group * (NY * CAP) + line] = product.astype(BF16)
         meta_ref[group, pl.ds(line, 1), :] = jnp.full((1, 128), label.astype(F32))
         return carry
 
-    lax.fori_loop(0, tiles_ref.shape[0], entry, 0, unroll=4)
+    lax.fori_loop(0, tiles_ref.shape[1], entry, 0, unroll=8)
 
 
 def map_tiles(focus_tiles, logits, focus_blocks):
@@ -315,7 +321,7 @@
         ],
         compiler_params=pltpu.CompilerParams(vmem_limit_bytes=VMEM_LIMIT),
         name="map_tiles",
-    )(focus_tiles, logits, focus_blocks)
+    )(focus_tiles.T, logits, focus_blocks)
 
 
 def exchange_kernel(
@@ -530,8 +536,7 @@
 
 
 def per_device(hidden_states, head_weight, focus_tiles, focus_blocks):
-    hidden = jnp.pad(hidden_states, ((0, 16 - hidden_states.shape[0]), (0, 0)))
-    logits = gather_logits(hidden, head_weight)
+    logits = gather_logits(hidden_states, head_weight)
     slots, meta = map_tiles(focus_tiles, logits, focus_blocks)
     return exchange(slots, meta)
 

time: 128 us -> 123 us (0.961)
  local copies, waits for them, and re-layouts: 4.67 us -> 1.92 us
  Pallas kernels: 123 us -> 121 us
    pallas_call x1, Pallas kernels: 7.75 us -> 6.13 us  [map_tiles(): pl.pallas_call(map_tiles_kernel, out_shape=(jax.ShapeDtypeStruct((groups...]
    pad x1 -> x0, local copies, waits for them, and re-layouts: 1.38 us -> none  [per_device(): hidden = jnp.pad(hidden_states, ((0, 16 - hidden_states.shape[0]), (0, 0)))]
    unnamed x2 -> x1, local copies, waits for them, and re-layouts: 3.29 us -> 1.92 us
where the time goes in v4:
time: 123 us
  Pallas kernels  121 us (98%)
  local copies, waits for them, and re-layouts  1.92 us (2%)
    pallas_call x1, Pallas kernels, gather_logits(): pl.pallas_call(gather_logits_kernel, out_shape=jax.ShapeDtypeStruct((96,...  62.7 us
    pallas_call x1, Pallas kernels, exchange(): pl.pallas_call(exchange_kernel, out_shape=jax.ShapeDtypeStruct((96, width...  52.3 us
    pallas_call x1, Pallas kernels, map_tiles(): pl.pallas_call(map_tiles_kernel, out_shape=(jax.ShapeDtypeStruct((groups...  6.13 us

profile of v4, /device:TPU:1, one launch (start us, length us, event | category | flops | bytes accessed | tf_op | source)
XLA Modules:
  0.0 123.1 jit_solution(4492633959964013555)
XLA Ops:
  0.0 62.7 %gather_logits.1.logits_ref = f32[96,1280]{1,0:T(8,128)} custom-call(bf16[12,1024]{1,0:T(8,128)(2,1)} %rows_ref.1, bf16[1024,1280]{1,0:T(8,128)(2,1)} %w_hbm.1), custom_call_target="tpu_custom_call" | custom-call | tf_op jit(solution)/shard_map/gather_logits/pallas_call | solution.py:221
  62.7 6.1 %map_tiles.1 = (bf16[128,96,128]{2,1,0:T(8,128)(2,1)}, f32[8,32,128]{2,1,0:T(8,128)}) custom-call(s32[2,64]{1,0:T(2,128)} %bitcast.1, f32[96,1280]{1,0:T(8,128)} %gather_logits.1.logits_ref, bf16[64,128,128]{2,1,0:T(8,128)(2,1)} %blocks_ref.1), custom_call_target="tpu_custom_call" | custom-call | tf_op jit(solution)/shard_map/map_tiles/pallas_call | solution.py:303
  68.9 52.3 %exchange.1 = f32[96,1536]{1,0:T(8,128)} custom-call(bf16[128,96,128]{2,1,0:T(8,128)(2,1)} %get-tuple-element.7.slots_hbm, f32[8,32,128]{2,1,0:T(8,128)} %get-tuple-element.8.meta_hbm), custom_call_target="tpu_custom_call" | custom-call | tf_op jit(solution)/shard_map/exchange/pallas_call | solution.py:513
  121.2 1.9 %copy.6 = f32[96,1536]{1,0:T(8,128)} copy(f32[96,1536]{1,0:T(8,128)} %exchange.1) | data formatting | bytes 1179648
